TPU v7x, 32 devices: a whole 2x2x4 slice. The times are simulated.
32 devices in a mesh: dp: 8 (over y, x, core), tensor: 4 (over z).
Axes of the slice: x: 2, y: 2, z: 4, core: 2. Of those that a mesh axis runs over, the one named last changes fastest.
Arguments:
- inputs: bfloat16 [8192, 1024], P(('dp', 'tensor')), may hold values from -6 to 6
- segments: int32 [8, 1024], P('dp'), may hold values from 0 to 3, never falling along the last dimension, each value on 1 to 512 neighbouring positions
- query_weight: bfloat16 [1024, 1024], P(None, 'tensor'), may hold values from -0.1875 to 0.1875
- key_weight: bfloat16 [1024, 1024], P(None, 'tensor'), may hold values from -0.1875 to 0.1875
- value_weight: bfloat16 [1024, 1024], P(None, 'tensor'), may hold values from -0.1875 to 0.1875
- gate_weight: bfloat16 [1024, 1024], P(None, 'tensor'), may hold values from -0.1875 to 0.1875
- out_weight: bfloat16 [1024, 1024], P('tensor'), may hold values from -0.1875 to 0.1875
- left_weight: bfloat16 [1024, 2816], P(None, 'tensor'), may hold values from -0.1875 to 0.1875
- right_weight: bfloat16 [1024, 2816], P(None, 'tensor'), may hold values from -0.1875 to 0.1875
- down_weight: bfloat16 [2816, 1024], P('tensor'), may hold values from -0.109375 to 0.109375
- norm_first: float32 [1024], replicated, may hold values from 0.1 to 1.9
- norm_second: float32 [1024], replicated, may hold values from 0.1 to 1.9
- cotangent: bfloat16 [8192, 1024], P(('dp', 'tensor')), may hold values from -6 to 6
Outputs:
- block_out: bfloat16 [8192, 1024], P(('dp', 'tensor'))
- block_grad: bfloat16 [8192, 1024], P(('dp', 'tensor'))
- query_grad: float32 [1024, 1024], P(None, 'tensor')
- key_grad: float32 [1024, 1024], P(None, 'tensor')
- value_grad: float32 [1024, 1024], P(None, 'tensor')
- gate_grad: float32 [1024, 1024], P(None, 'tensor')
- out_grad: float32 [1024, 1024], P('tensor')
- left_grad: float32 [1024, 2816], P(None, 'tensor')
- right_grad: float32 [1024, 2816], P(None, 'tensor')
- down_grad: float32 [2816, 1024], P('tensor')
- first_grad: float32 [1024], replicated
- second_grad: float32 [1024], replicated
Inputs may be any that keep to these rules, and one draw needn't show every extreme that they name: `segments`: each row holds 4 documents; numbers never fall along a row; each document has 1 to 512 tokens and one of each row exactly 512.
All inputs are finite; a program needn't handle non-finite values.
Results may differ from a plain program's by a relative error of at most 0.02.
Values may be sent and summed in bfloat16 or wider, within the bound.
A program may use at most 128 MiB of HBM per device.

v0:
```python
import jax
import jax.numpy as jnp
from jax import lax
from jax.sharding import PartitionSpec as P

D = 1024
HEADS = 16
EPS = 1e-05


def rms_scale(values):
    return lax.rsqrt(jnp.mean(values * values, axis=-1, keepdims=True) + EPS)


def norm_back(grad_normed, values, scale, gain):
    weighted = grad_normed * gain
    return scale * weighted - values * scale * scale * scale * jnp.mean(
        weighted * values, axis=-1, keepdims=True
    )


def attention_scores(query_pos, key_pos, doc_mask):
    raw_scores = jnp.einsum(
        "rthd,rshd->rhts", query_pos, key_pos, preferred_element_type=jnp.float32
    )
    return jnp.where(doc_mask[:, None], raw_scores, 0.0).astype(jnp.bfloat16)


def per_device(
    inputs,
    segments,
    query_weight,
    key_weight,
    value_weight,
    gate_weight,
    out_weight,
    left_weight,
    right_weight,
    down_weight,
    norm_first,
    norm_second,
    cotangent,
):
    own_rows = inputs.astype(jnp.float32)
    rows_here, length = segments.shape
    all_tokens = rows_here * length
    local_width = query_weight.shape[1]
    head_size = D // HEADS
    heads_here = local_width // head_size
    four_shape = (rows_here, length, heads_here, head_size)
    scale_one = rms_scale(own_rows)
    normed_own = (own_rows * scale_one * norm_first).astype(jnp.bfloat16)
    normed_all = lax.all_gather(normed_own, "tensor", axis=0, tiled=True)
    joined_weight = jnp.concatenate((query_weight, key_weight, value_weight, gate_weight), axis=1)
    projected = jnp.dot(normed_all, joined_weight, preferred_element_type=jnp.float32)
    query_raw = projected[:, :local_width]
    key_raw = projected[:, local_width : 2 * local_width]
    value_raw = projected[:, 2 * local_width : 3 * local_width]
    gate_raw = projected[:, 3 * local_width :]
    query_pos = jax.nn.softplus(query_raw).astype(jnp.bfloat16).reshape(four_shape)
    key_pos = jax.nn.softplus(key_raw).astype(jnp.bfloat16).reshape(four_shape)
    value_pos = value_raw.astype(jnp.bfloat16).reshape(four_shape)
    later = lax.broadcasted_iota(jnp.int32, (length, length), 0) >= lax.broadcasted_iota(
        jnp.int32, (length, length), 1
    )
    doc_mask = (segments[:, :, None] == segments[:, None, :]) & later[None]
    scores = attention_scores(query_pos, key_pos, doc_mask)
    mixed_heads = jnp.einsum(
        "rhts,rshd->rthd", scores, value_pos, preferred_element_type=jnp.float32
    )
    head_scale = rms_scale(mixed_heads)
    head_norm = (mixed_heads * head_scale).reshape(all_tokens, local_width)
    gate_open = jax.nn.sigmoid(gate_raw)
    gated = (head_norm * gate_open).astype(jnp.bfloat16)
    branch = lax.psum_scatter(
        jnp.dot(gated, out_weight, preferred_element_type=jnp.float32).astype(jnp.bfloat16),
        "tensor",
        scatter_dimension=0,
        tiled=True,
    ).astype(jnp.float32)
    residual = own_rows + branch
    scale_two = rms_scale(residual)
    second_own = (residual * scale_two * norm_second).astype(jnp.bfloat16)
    second_all = lax.all_gather(second_own, "tensor", axis=0, tiled=True)
    left_out = jnp.dot(second_all, left_weight, preferred_element_type=jnp.float32)
    right_out = jnp.dot(second_all, right_weight, preferred_element_type=jnp.float32)
    product = (left_out * right_out).astype(jnp.bfloat16)
    ffn_share = lax.psum_scatter(
        jnp.dot(product, down_weight, preferred_element_type=jnp.float32).astype(jnp.bfloat16),
        "tensor",
        scatter_dimension=0,
        tiled=True,
    ).astype(jnp.float32)
    block_out = (residual + ffn_share).astype(jnp.bfloat16)
    upstream = cotangent.astype(jnp.float32)
    down_in = lax.all_gather(cotangent, "tensor", axis=0, tiled=True)
    down_grad = jnp.einsum("tf,td->fd", product, down_in, preferred_element_type=jnp.float32)
    prod_grad = jnp.einsum("td,fd->tf", down_in, down_weight, preferred_element_type=jnp.float32)
    left_back = (prod_grad * right_out).astype(jnp.bfloat16)
    right_back = (prod_grad * left_out).astype(jnp.bfloat16)
    left_grad = jnp.einsum("tc,tf->cf", second_all, left_back, preferred_element_type=jnp.float32)
    right_grad = jnp.einsum("tc,tf->cf", second_all, right_back, preferred_element_type=jnp.float32)
    second_back = lax.psum_scatter(
        (
            jnp.einsum("tf,cf->tc", left_back, left_weight, preferred_element_type=jnp.float32)
            + jnp.einsum("tf,cf->tc", right_back, right_weight, preferred_element_type=jnp.float32)
        ).astype(jnp.bfloat16),
        "tensor",
        scatter_dimension=0,
        tiled=True,
    ).astype(jnp.float32)
    second_part = jnp.sum(second_back * residual * scale_two, axis=0)
    resid_grad = upstream + norm_back(second_back, residual, scale_two, norm_second)
    mixer_in = lax.all_gather(resid_grad.astype(jnp.bfloat16), "tensor", axis=0, tiled=True)
    out_grad = jnp.einsum("tc,td->cd", gated, mixer_in, preferred_element_type=jnp.float32)
    gated_back = jnp.einsum("td,cd->tc", mixer_in, out_weight, preferred_element_type=jnp.float32)
    gate_back = (gated_back * head_norm * gate_open * (1.0 - gate_open)).astype(jnp.bfloat16)
    norm_grad = (gated_back * gate_open).reshape(four_shape)
    mixed_back = (
        head_scale * norm_grad
        - mixed_heads
        * head_scale
        * head_scale
        * head_scale
        * jnp.mean(norm_grad * mixed_heads, axis=-1, keepdims=True)
    ).astype(jnp.bfloat16)
    scores_again = attention_scores(query_pos, key_pos, doc_mask)
    value_back = jnp.einsum(
        "rhts,rthd->rshd", scores_again, mixed_back, preferred_element_type=jnp.float32
    ).astype(jnp.bfloat16)
    score_back = jnp.einsum(
        "rthd,rshd->rhts", mixed_back, value_pos, preferred_element_type=jnp.float32
    )
    score_back = jnp.where(doc_mask[:, None], score_back, 0.0).astype(jnp.bfloat16)
    query_back = jnp.einsum(
        "rhts,rshd->rthd", score_back, key_pos, preferred_element_type=jnp.float32
    )
    query_back = (query_back * jax.nn.sigmoid(query_raw.reshape(four_shape))).astype(jnp.bfloat16)
    key_back = jnp.einsum(
        "rhts,rthd->rshd", score_back, query_pos, preferred_element_type=jnp.float32
    )
    key_back = (key_back * jax.nn.sigmoid(key_raw.reshape(four_shape))).astype(jnp.bfloat16)
    back_all = jnp.concatenate(
        (
            query_back.reshape(all_tokens, local_width),
            key_back.reshape(all_tokens, local_width),
            value_back.reshape(all_tokens, local_width),
            gate_back,
        ),
        axis=1,
    )
    joined_grad = jnp.einsum("tc,tq->cq", normed_all, back_all, preferred_element_type=jnp.float32)
    query_grad = joined_grad[:, :local_width]
    key_grad = joined_grad[:, local_width : 2 * local_width]
    value_grad = joined_grad[:, 2 * local_width : 3 * local_width]
    gate_grad = joined_grad[:, 3 * local_width :]
    first_back = lax.psum_scatter(
        jnp.einsum("tq,cq->tc", back_all, joined_weight, preferred_element_type=jnp.float32).astype(
            jnp.bfloat16
        ),
        "tensor",
        scatter_dimension=0,
        tiled=True,
    ).astype(jnp.float32)
    first_part = jnp.sum(first_back * own_rows * scale_one, axis=0)
    block_grad = (resid_grad + norm_back(first_back, own_rows, scale_one, norm_first)).astype(
        jnp.bfloat16
    )
    query_grad, key_grad, value_grad, gate_grad, out_grad, left_grad, right_grad, down_grad = (
        total.astype(jnp.float32)
        for total in lax.psum(
            tuple(
                (
                    part.astype(jnp.bfloat16)
                    for part in (
                        query_grad,
                        key_grad,
                        value_grad,
                        gate_grad,
                        out_grad,
                        left_grad,
                        right_grad,
                        down_grad,
                    )
                )
            ),
            "dp",
        )
    )
    first_grad, second_grad = lax.psum((first_part, second_part), ("dp", "tensor"))
    return (
        block_out,
        block_grad,
        query_grad,
        key_grad,
        value_grad,
        gate_grad,
        out_grad,
        left_grad,
        right_grad,
        down_grad,
        first_grad,
        second_grad,
    )


def solution(mesh):
    return jax.shard_map(
        per_device,
        mesh=mesh,
        in_specs=(
            P(("dp", "tensor"), None),
            P("dp", None),
            P(None, "tensor"),
            P(None, "tensor"),
            P(None, "tensor"),
            P(None, "tensor"),
            P("tensor", None),
            P(None, "tensor"),
            P(None, "tensor"),
            P("tensor", None),
            P(),
            P(),
            P(("dp", "tensor"), None),
        ),
        out_specs=(
            P(("dp", "tensor"), None),
            P(("dp", "tensor"), None),
            P(None, "tensor"),
            P(None, "tensor"),
            P(None, "tensor"),
            P(None, "tensor"),
            P("tensor", None),
            P(None, "tensor"),
            P(None, "tensor"),
            P("tensor", None),
            P(),
            P(),
        ),
        check_vma=False,
    )
```

profile of v0, /device:TPU:0, one launch (start us, length us, event | category | flops | bytes accessed | tf_op | source)
XLA Modules:
  0.0 557.3 jit_solution(13068382878314407634)
XLA Ops:
  7.3 1.4 fusion.21
  8.7 0.6 copy-done.43
  9.2 2.0 fusion.10
  11.6 0.7 copy-done.33
  12.4 1.3 copy-done.35
  13.7 0.6 fusion
  14.3 45.8 %all-gather.5.cloned.1.call-done = bf16[1024,1024]{1,0:T(8,128)(2,1)} async-done(((bf16[256,1024]{1,0:T(8,128)(2,1)}), bf16[1024,1024]{1,0:T(8,128)(2,1)}) %all-gather.5.cloned.1.call-update) | async-done | bytes 2097168 | tf_op jit(solution)/shard_map/all_gather | solution.py:53
  60.1 4.7 fusion.40
  64.9 1.1 fusion.26
  66.1 2.6 select_convert_fusion.1
  68.8 2.7 multiply_reduce_fusion.2
  71.5 0.6 copy-done.1
  72.2 1.0 copy-done.11
  73.1 0.3 fusion.30
  73.5 0.8 copy-done.15
  74.3 2.1 convolution_convert_fusion.2
  76.4 42.7 %reduce-scatter.5.cloned.1.call-done = bf16[256,1024]{1,0:T(8,128)(2,1)} async-done(((bf16[1024,1024]{1,0:T(8,128)(2,1)}), bf16[256,1024]{1,0:T(8,128)(2,1)}) %reduce-scatter.5.cloned.1.call-update) | async-done | bytes 524304 | tf_op jit(solution)/shard_map/reduce_scatter | solution.py:75
  119.1 1.3 multiply_reduce_fusion.1
  120.4 2.0 multiply_convert_fusion.3
  122.5 0.5 all-gather.9.cloned.1.call-update
  123.0 0.5 reduce-scatter.9.cloned.1.call-start
  123.6 44.3 %all-gather.7.cloned.1.call-done = bf16[1024,1024]{1,0:T(8,128)(2,1)} async-done(((bf16[256,1024]{1,0:T(8,128)(2,1)}), bf16[1024,1024]{1,0:T(8,128)(2,1)}) %all-gather.7.cloned.1.call-update) | async-done | bytes 2097168 | tf_op jit(solution)/shard_map/all_gather | solution.py:84
  167.9 5.4 fusion.42
  173.3 3.3 fusion.41
  176.6 37.5 %all-gather.9.cloned.1.call-done = bf16[1024,1024]{1,0:T(8,128)(2,1)} async-done(((bf16[256,1024]{1,0:T(8,128)(2,1)}), bf16[1024,1024]{1,0:T(8,128)(2,1)}) %all-gather.9.cloned.1.call-update) | async-done | bytes 2097168 | tf_op jit(solution)/shard_map/all_gather | solution.py:96
  214.1 6.3 %multiply_convert_fusion = (bf16[1024,704]{0,1:T(8,128)(2,1)S(1)}, bf16[1024,704]{0,1:T(8,128)(2,1)}, bf16[1024,704]{0,1:T(8,128)(2,1)S(1)}) fusion(f32[1024,704]{0,1:T(8,128)} %fusion.41, f32[1024,704]{0,1:T(8,128)} %fusion.42, bf16[1024,1024]{1,0:T(8,128)(2,1)} %all-gather.9.cloned.1.call-done, bf16[704,1024]{1,0:T(8,128)(2,1)S(1)} %copy-done), kind=kOutput, calls=%fused_computation.7 | convolution fusion | flops 1480720384 | bytes 13631488 | tf_op jit(solution)/shard_map/td,fd->tf/dot_general | solution.py:98
  220.5 1.8 fusion.43
  222.3 0.5 copy-done.51
  222.9 3.2 add_convert_fusion
  226.1 42.7 %reduce-scatter.9.cloned.1.call-done = bf16[256,1024]{1,0:T(8,128)(2,1)} async-done(((bf16[1024,1024]{1,0:T(8,128)(2,1)}), bf16[256,1024]{1,0:T(8,128)(2,1)}) %reduce-scatter.9.cloned.1.call-update) | async-done | bytes 524304 | tf_op jit(solution)/shard_map/reduce_scatter | solution.py:103
  268.8 2.0 fusion.20
  270.8 0.6 copy-done.44
  271.4 2.5 fusion.37
  274.2 4.9 convolution_convert_fusion.4
  279.1 2.8 convolution_convert_fusion.5
  281.9 2.8 convolution_convert_fusion.6
  284.7 34.7 %all-gather.11.cloned.1.call-done = bf16[1024,1024]{1,0:T(8,128)(2,1)} async-done(((bf16[256,1024]{1,0:T(8,128)(2,1)}), bf16[1024,1024]{1,0:T(8,128)(2,1)}) %all-gather.11.cloned.1.call-update) | async-done | bytes 2097168 | tf_op jit(solution)/shard_map/all_gather | solution.py:114
  319.3 4.1 fusion.38
  323.7 0.3 fusion.34
  324.0 5.1 convolution_convert_fusion.7
  329.1 2.7 select_convert_fusion
  331.8 1.6 fusion.4
  333.4 2.9 fusion.3
  336.3 2.4 convolution_convert_fusion
  338.7 1.4 fusion.39
  340.1 1.1 copy-done.48
  341.2 1.5 convolution_convert_fusion.8
  342.8 5.6 %convolution_convert_fusion.1 = bf16[1024,1024]{1,0:T(8,128)(2,1)} fusion(bf16[1024,1024]{1,0:T(8,128)(2,1)} %copy-done.35, bf16[1024,256]{0,1:T(8,128)(2,1)} %copy-done.52, bf16[1024,256]{0,1:T(8,128)(2,1)S(1)} %bitcast.98, bf16[1024,256]{0,1:T(8,128)(2,1)S(1)} %bitcast.100, bf16[1024,256]{0,1:T(8,128)(2,1)} %bitcast.102), kind=kOutput, calls=%fused_computation.17 | convolution fusion | flops 2156920832 | bytes 6291456 | tf_op jit(solution)/shard_map/tq,cq->tc/dot_general | solution.py:158
  348.6 4.6 convolution_convert_fusion.3
  353.2 101.3 %all-reduce.4.cloned.1.call-done = (bf16[1024,256]{1,0:T(8,128)(2,1)}, bf16[1024,256]{1,0:T(8,128)(2,1)}, bf16[1024,256]{1,0:T(8,128)(2,1)}, bf16[1024,256]{1,0:...) async-done(((bf16[1024,256]{1,0:T(8,128)(2,1)}, bf16[1024,256]{1,0:T(8,128)(2,1)}, ...) | async-done | bytes 6946832 | tf_op jit(solution)/shard_map/psum | solution.py:171
  454.5 2.2 convert_element_type.164
  456.6 2.1 convert_element_type.165
  458.8 1.0 convert_element_type.166
  459.8 1.0 convert_element_type.167
  460.9 1.1 convert_element_type.169
  462.0 1.9 convert_element_type.171
  463.9 1.9 convert_element_type.173
  465.9 1.9 convert_element_type.175
  467.9 33.0 %reduce-scatter.11.cloned.1.call-done = bf16[256,1024]{1,0:T(8,128)(2,1)} async-done(((bf16[1024,1024]{1,0:T(8,128)(2,1)}), bf16[256,1024]{1,0:T(8,128)(2,1)}) %reduce-scatter.11.cloned.1.call-update) | async-done | bytes 524304 | tf_op jit(solution)/shard_map/reduce_scatter | solution.py:157
  500.8 2.0 fusion.24
  502.8 42.2 %all-reduce = (f32[1024]{0:T(1024)}, f32[1024]{0:T(1024)}) all-reduce(f32[1024]{0:T(1024)} %get-tuple-element.14, f32[1024]{0:T(1024)S(1)} %copy-done.42), channel_id=1, replica_groups=mesh['dp'=8,'tensor'=4] {'dp','tensor'}, use_global_device_ids=true, to_apply=%region_19.20 | all-reduce | flops 2048 | bytes 16384 | tf_op jit(solution)/shard_map/psum | solution.py:190
  545.0 0.7 broadcast_multiply_fusion.2
  545.7 1.7 reduce-scatter.7.cloned.1.call-done
  547.4 3.1 fusion.15
  (125 shorter events, 1.6 us)
Async XLA Ops:
  7.2 206.9 %copy-start = (bf16[704,1024]{1,0:T(8,128)(2,1)S(1)}, bf16[704,1024]{1,0:T(8,128)(2,1)}, u32[]{:S(2)}) copy-start(bf16[704,1024]{1,0:T(8,128)(2,1)} %param.22) | copy-start | bytes 4325380
  7.2 4.2 copy-start.30
  7.2 4.2 copy-start.31
  7.2 4.3 copy-start.32
  7.2 52.9 %all-gather.5.cloned.1.call-start = ((), (), s32[]{:S(2)}) async-start(), calls=%async_computation.4 | async-start | bytes 2621440 | tf_op jit(solution)/shard_map/all_gather | solution.py:53
  8.7 0.6 copy-start.43
  11.3 1.0 copy-start.33
  11.3 2.4 copy-start.41
  11.3 107.8 %reduce-scatter.5.cloned.1.call-start = ((), (), s32[]{:S(2)}) async-start(), calls=%async_computation.5 | async-start | bytes 2621440 | tf_op jit(solution)/shard_map/reduce_scatter | solution.py:75
  12.4 1.3 copy-start.35
  14.3 51.7 %copy-start.24 = (pred[1024,1024]{1,0:T(8,128)(4,1)}, pred[1024,1024]{1,0:T(8,128)(4,1)S(1)}, u32[]{:S(2)}) copy-start(pred[1024,1024]{1,0:T(8,128)(4,1)S(1)} %fusion) | copy-start | bytes 3145732
  64.8 7.4 %copy-start.12 = (f32[1024,1024]{0,1:T(8,128)}, f32[1024,1024]{0,1:T(8,128)S(1)}, u32[]{:S(2)}) copy-start(f32[1024,1024]{0,1:T(8,128)S(1)} %fusion.40) | copy-start | bytes 12582916
  64.9 3.9 copy-start.13
  66.0 2.7 copy-start.17
  66.0 2.7 copy-start.19
  68.7 3.3 copy-start.1
  72.0 2.2 copy-start.34
  72.2 1.0 copy-start.11
  73.5 0.8 copy-start.15
  74.3 44.8 %copy-start.2 = (bf16[256,1024]{1,0:T(8,128)(2,1)S(1)}, bf16[256,1024]{1,0:T(8,128)(2,1)}, u32[]{:S(2)}) copy-start(bf16[256,1024]{1,0:T(8,128)(2,1)} %param.13) | copy-start | bytes 1572868
  76.3 44.1 %copy-start.36 = (f32[1024]{0:T(1024)S(1)}, f32[1024]{0:T(1024)}, u32[]{:S(2)}) copy-start(f32[1024]{0:T(1024)} %param.24) | copy-start | bytes 12292
  76.4 91.5 %all-gather.7.cloned.1.call-start = ((), (), s32[]{:S(2)}) async-start(), calls=%async_computation.6 | async-start | bytes 2621440 | tf_op jit(solution)/shard_map/all_gather | solution.py:84
  120.4 52.9 %copy-start.39 = (f32[256]{0:T(256)}, f32[256]{0:T(256)S(1)}, u32[]{:S(2)}) copy-start(f32[256]{0:T(256)S(1)} %add_rsqrt_fusion.1) | copy-start | bytes 3076
  122.5 91.6 %all-gather.9.cloned.1.call-start = ((), (), s32[]{:S(2)}) async-start(), calls=%async_computation.8 | async-start | bytes 2621440 | tf_op jit(solution)/shard_map/all_gather | solution.py:96
  123.0 145.8 %reduce-scatter.9.cloned.1.call-start = ((), (), s32[]{:S(2)}) async-start(), calls=%async_computation.9 | async-start | bytes 2621440 | tf_op jit(solution)/shard_map/reduce_scatter | solution.py:103
  167.9 5.4 copy-start.46
  167.9 5.4 copy-start.49
  214.1 6.4 %copy-start.50 = (bf16[1024,704]{0,1:T(8,128)(2,1)S(1)}, bf16[1024,704]{0,1:T(8,128)(2,1)}, u32[]{:S(2)}) copy-start(bf16[1024,704]{0,1:T(8,128)(2,1)} %param.20) | copy-start | bytes 4325380
  220.4 1.9 copy-start.8
  220.4 1.9 copy-start.10
  220.4 2.4 copy-start.51
  226.0 42.8 %copy-start.3 = (bf16[256,1024]{1,0:T(8,128)(2,1)S(1)}, bf16[256,1024]{1,0:T(8,128)(2,1)}, u32[]{:S(2)}) copy-start(bf16[256,1024]{1,0:T(8,128)(2,1)} %reduce-scatter.5.cloned.1.call-done) | copy-start | bytes 1572868
  226.1 93.3 %all-gather.11.cloned.1.call-start = ((), (), s32[]{:S(2)}) async-start(), calls=%async_computation.10 | async-start | bytes 2621440 | tf_op jit(solution)/shard_map/all_gather | solution.py:114
  270.8 0.6 copy-start.44
  273.9 180.5 %all-reduce.4.cloned.1.call-start = ((), (), s32[]{:S(2)}) async-start(), calls=%async_computation.12 | async-start | bytes 13893632 | tf_op jit(solution)/shard_map/psum | solution.py:171
  274.2 5.0 copy-start.9
  274.2 5.0 copy-start.47
  279.1 2.8 copy-start.4
  279.1 2.8 copy-start.7
  323.4 12.9 %copy-start.52 = (bf16[1024,256]{0,1:T(8,128)(2,1)}, bf16[1024,256]{0,1:T(8,128)(2,1)S(1)}, u32[]{:S(2)}) copy-start(bf16[1024,256]{0,1:T(8,128)(2,1)S(1)} %get-tuple-element.27) | copy-start | bytes 1572868
  323.9 5.1 copy-start.14
  324.0 5.1 copy-start.25
  329.1 2.7 copy-start.20
  331.8 1.6 copy-start.18
  333.4 2.9 copy-start.45
  336.3 2.4 copy-start.29
  338.7 1.4 copy-start.16
  338.7 2.5 copy-start.48
  342.8 158.1 %reduce-scatter.11.cloned.1.call-start = ((), (), s32[]{:S(2)}) async-start(), calls=%async_computation.11 | async-start | bytes 2621440 | tf_op jit(solution)/shard_map/reduce_scatter | solution.py:157
  348.5 198.9 %reduce-scatter.7.cloned.1.call-start = ((), (), s32[]{:S(2)}) async-start(), calls=%async_computation.7 | async-start | bytes 2621440 | tf_op jit(solution)/shard_map/reduce_scatter | solution.py:88
  454.5 4.3 copy-start.28
  454.5 5.4 copy-start.27
  456.6 4.2 copy-start.26
  458.8 3.2 copy-start.23
  462.0 2.0 copy-start.22
  463.9 1.9 copy-start.21
  465.9 35.0 %copy-start.38 = (f32[1024]{0:T(1024)S(1)}, f32[1024]{0:T(1024)}, u32[]{:S(2)}) copy-start(f32[1024]{0:T(1024)} %param.23) | copy-start | bytes 12292
  465.9 36.9 %copy-start.42 = (f32[1024]{0:T(1024)S(1)}, f32[1024]{0:T(1024)}, u32[]{:S(2)}) copy-start(f32[1024]{0:T(1024)} %get-tuple-element.12) | copy-start | bytes 12292
  465.9 81.5 %copy-start.5 = (bf16[256,1024]{1,0:T(8,128)(2,1)S(1)}, bf16[256,1024]{1,0:T(8,128)(2,1)}, u32[]{:S(2)}) copy-start(bf16[256,1024]{1,0:T(8,128)(2,1)} %param.25) | copy-start | bytes 1572868
  465.9 81.5 %copy-start.6 = (bf16[256,1024]{1,0:T(8,128)(2,1)S(1)}, bf16[256,1024]{1,0:T(8,128)(2,1)}, u32[]{:S(2)}) copy-start(bf16[256,1024]{1,0:T(8,128)(2,1)} %reduce-scatter.9.cloned.1.call-done) | copy-start | bytes 1572868
  465.9 81.5 %copy-start.37 = (f32[1024]{0:T(1024)S(1)}, f32[1024]{0:T(1024)}, u32[]{:S(2)}) copy-start(f32[1024]{0:T(1024)} %param.24) | copy-start | bytes 12292
  465.9 81.5 %copy-start.40 = (f32[256]{0:T(256)S(1)}, f32[256]{0:T(256)}, u32[]{:S(2)}) copy-start(f32[256]{0:T(256)} %copy-done.39) | copy-start | bytes 3076
Sparse Core Ops, SparseCore 0:
  11.4 48.6 all-gather.4
  76.5 42.5 reduce-scatter.4
  122.6 45.2 all-gather.6
  169.4 44.6 all-gather.8
  226.2 42.5 reduce-scatter.8
  274.1 45.2 all-gather.10
  342.9 111.5 all-reduce.3
  456.8 43.9 reduce-scatter.10
  503.1 44.1 reduce-scatter.6
where the time goes:
time: 566 us; the launch traced here: 557 us
  waiting for transfers between devices  384 us (68%)
  matrix products  73 us (13%)
  blocking collectives  42.2 us (7%)
  other arithmetic  33 us (6%)
  between operations  14.7 us (3%)
  local copies, waits for them, and re-layouts  9.13 us (2%)
    psum x1, waiting for transfers between devices, per_device(): lax.psum(tuple((part.astype(jnp.bfloat16) for part in (query_grad, key_gr...  101 us
    all_gather x1, waiting for transfers between devices, per_device(): normed_all = lax.all_gather(normed_own, 'tensor', axis=0, tiled=True)  45.8 us
    all_gather x1, waiting for transfers between devices, per_device(): second_all = lax.all_gather(second_own, 'tensor', axis=0, tiled=True)  44.3 us
    reduce_scatter x1, waiting for transfers between devices, per_device(): lax.psum_scatter((jnp.einsum('tf,cf->tc', left_back, left_weight, preferr...  42.7 us
    reduce_scatter x1, waiting for transfers between devices, per_device(): lax.psum_scatter(jnp.dot(gated, out_weight, preferred_element_type=jnp.fl...  42.7 us
    psum x1, blocking collectives, per_device(): lax.psum((first_part, second_part), ('dp', 'tensor'))  42.2 us
    all_gather x1, waiting for transfers between devices, per_device(): down_in = lax.all_gather(cotangent, 'tensor', axis=0, tiled=True)  37.5 us
    all_gather x1, waiting for transfers between devices, per_device(): lax.all_gather(resid_grad.astype(jnp.bfloat16), 'tensor', axis=0, tiled=T...  34.7 us
  transfers between devices with their start and end apart: 9, of which 9 were waited for; matrix products, arithmetic and copies ran while one was open for 8% of the time, Pallas kernels for 0%

commit v1 on v0

--- a/solution.py
+++ b/solution.py
@@ -81,7 +81,14 @@
     residual = own_rows + branch
     scale_two = rms_scale(residual)
     second_own = (residual * scale_two * norm_second).astype(jnp.bfloat16)
-    second_all = lax.all_gather(second_own, "tensor", axis=0, tiled=True)
+    ring = [second_own]
+    for hop in range(3):
+        ring.append(lax.ppermute(ring[-1], "tensor", [(dev, (dev + 1) % 4) for dev in range(4)]))
+    second_all = jnp.roll(
+        jnp.concatenate(ring[::-1], axis=0),
+        (lax.axis_index("tensor") + 1) * ring[0].shape[0],
+        axis=0,
+    )
     left_out = jnp.dot(second_all, left_weight, preferred_element_type=jnp.float32)
     right_out = jnp.dot(second_all, right_weight, preferred_element_type=jnp.float32)
     product = (left_out * right_out).astype(jnp.bfloat16)

time: 566 us -> 548 us (0.968)
  waiting for transfers between devices: 384 us -> 353 us
  starting transfers between devices: 1.01 us -> 14.8 us
  matrix products: 73 us -> 66 us
  local copies, waits for them, and re-layouts: 9.13 us -> 15.6 us
    ppermute x0 -> x3, waiting for transfers between devices: none -> 51.2 us  [per_device(): lax.ppermute(ring[-1], 'tensor', [(dev, (dev + 1) % 4) for dev in range(4)])]
    all_gather x1 -> x0, waiting for transfers between devices: 44.3 us -> none  [per_device(): second_all = lax.all_gather(second_own, 'tensor', axis=0, tiled=True)]
    all_gather x1, waiting for transfers between devices: 37.5 us -> 1.88 us  [per_device(): down_in = lax.all_gather(cotangent, 'tensor', axis=0, tiled=True)]
    ppermute x0 -> x3, starting transfers between devices: none -> 14.3 us  [per_device(): lax.ppermute(ring[-1], 'tensor', [(dev, (dev + 1) % 4) for dev in range(4)])]
    unnamed x109 -> x126, local copies, waits for them, and re-layouts: 7.62 us -> 14 us
  transfers between devices with their start and end apart: 9 -> 11, of which waited for: 9 -> 11; matrix products, arithmetic and copies ran while one was open for 8% -> 8% of each run, Pallas kernels for 0% -> 0%
where the time goes in v1:
time: 548 us; the launch traced here: 539 us
  waiting for transfers between devices  353 us (64%)
  matrix products  66 us (12%)
  blocking collectives  42.2 us (8%)
  other arithmetic  32.1 us (6%)
  local copies, waits for them, and re-layouts  15.6 us (3%)
  between operations  15.1 us (3%)
  starting transfers between devices  14.8 us (3%)
    psum x1, waiting for transfers between devices, per_device(): lax.psum(tuple((part.astype(jnp.bfloat16) for part in (query_grad, key_gr...  99.4 us
    ppermute x3, waiting for transfers between devices, per_device(): lax.ppermute(ring[-1], 'tensor', [(dev, (dev + 1) % 4) for dev in range(4)])  51.2 us
    all_gather x1, waiting for transfers between devices, per_device(): normed_all = lax.all_gather(normed_own, 'tensor', axis=0, tiled=True)  45.8 us
    reduce_scatter x1, waiting for transfers between devices, per_device(): lax.psum_scatter((jnp.einsum('tf,cf->tc', left_back, left_weight, preferr...  43 us
    psum x1, blocking collectives, per_device(): lax.psum((first_part, second_part), ('dp', 'tensor'))  42.2 us
    reduce_scatter x1, waiting for transfers between devices, per_device(): lax.psum_scatter(jnp.dot(gated, out_weight, preferred_element_type=jnp.fl...  42 us
    all_gather x1, waiting for transfers between devices, per_device(): lax.all_gather(resid_grad.astype(jnp.bfloat16), 'tensor', axis=0, tiled=T...  34.6 us
    reduce_scatter x1, waiting for transfers between devices, per_device(): lax.psum_scatter(jnp.einsum('tq,cq->tc', back_all, joined_weight, preferr...  32.9 us
  transfers between devices with their start and end apart: 11, of which 11 were waited for; matrix products, arithmetic and copies ran while one was open for 8% of the time, Pallas kernels for 0%

profile of v1, /device:TPU:0, one launch (start us, length us, event | category | flops | bytes accessed | tf_op | source)
XLA Modules:
  0.0 538.9 jit_solution(3036371020690239767)
XLA Ops:
  7.3 1.4 fusion.27
  9.3 2.0 fusion.16
  12.4 1.3 copy-done.41
  14.3 45.8 %all-gather.4.cloned.1.call-done = bf16[1024,1024]{1,0:T(8,128)(2,1)} async-done(((bf16[256,1024]{1,0:T(8,128)(2,1)}), bf16[1024,1024]{1,0:T(8,128)(2,1)}) %all-gather.4.cloned.1.call-update) | async-done | bytes 2097168 | tf_op jit(solution)/shard_map/all_gather | solution.py:53
  60.1 4.7 fusion.50
  64.9 1.1 fusion.32
  66.1 2.6 select_convert_fusion.1
  68.8 2.7 multiply_reduce_fusion.2
  73.2 0.8 copy-done.13
  74.0 2.1 convolution_convert_fusion.2
  76.8 42.0 %reduce-scatter.5.cloned.1.call-done = bf16[256,1024]{1,0:T(8,128)(2,1)} async-done(((bf16[1024,1024]{1,0:T(8,128)(2,1)}), bf16[256,1024]{1,0:T(8,128)(2,1)}) %reduce-scatter.5.cloned.1.call-update) | async-done | bytes 524304 | tf_op jit(solution)/shard_map/reduce_scatter | solution.py:75
  118.8 1.3 multiply_reduce_fusion.1
  120.1 1.2 multiply_convert_fusion.3
  121.4 21.3 %collective-permute-done = bf16[256,1024]{1,0:T(8,128)(2,1)S(1)} collective-permute-done((bf16[256,1024]{1,0:T(8,128)(2,1)S(1)}, bf16[256,1024]{1,0:T(8,128)(2,1)S(1)}, u32[]{:S(2)}, u32[]{:S(2)}) %collective-permute-start) | collective-permute-done | bytes 524320 | tf_op jit(solution)/shard_map/ppermute | solution.py:86
  142.7 0.8 copy-done.19
  143.5 3.8 collective-permute-start.1
  147.3 22.6 %collective-permute-done.1 = bf16[256,1024]{1,0:T(8,128)(2,1)} collective-permute-done((bf16[256,1024]{1,0:T(8,128)(2,1)S(1)}, bf16[256,1024]{1,0:T(8,128)(2,1)}, u32[]{:S(2)}, u32[]{:S(2)}) %collective-permute-start.1) | collective-permute-done | bytes 524320 | tf_op jit(solution)/shard_map/ppermute | solution.py:86
  169.9 10.4 %collective-permute-start.2 = (bf16[256,1024]{1,0:T(8,128)(2,1)}, bf16[256,1024]{1,0:T(8,128)(2,1)}, u32[]{:S(2)}, u32[]{:S(2)}) collective-permute-start(bf16[256,1024]{1,0:T(8,128)(2,1)} %collective-permute-done.1), channel_id=1, source_target_pairs={{0,1},{1,2},{2,3},{3,0},{4,5},{5,6},{6,7},{7,4},{8,9},{9,10},{10,1... | collective-permute-start | bytes 1572872 | tf_op jit(solution)/shard_map/ppermute | solution.py:86
  180.4 1.9 all-gather.6.cloned.1.call-done
  182.2 3.7 fusion.51
  185.9 7.3 %collective-permute-done.2 = bf16[256,1024]{1,0:T(8,128)(2,1)} collective-permute-done((bf16[256,1024]{1,0:T(8,128)(2,1)}, bf16[256,1024]{1,0:T(8,128)(2,1)}, u32[]{:S(2)}, u32[]{:S(2)}) %collective-permute-start.2) | collective-permute-done | bytes 524320 | tf_op jit(solution)/shard_map/ppermute | solution.py:86
  193.3 1.1 constant_dynamic-update-slice_fusion.11
  194.3 1.1 constant_dynamic-update-slice_fusion.10
  195.5 1.2 constant_dynamic-update-slice_fusion.7
  196.7 1.1 constant_dynamic-update-slice_fusion.6
  197.9 1.7 fusion.5
  199.8 3.0 multiply_convert_fusion
  202.9 1.9 fusion.52
  204.8 3.3 add_convert_fusion
  208.1 43.0 %reduce-scatter.9.cloned.1.call-done = bf16[256,1024]{1,0:T(8,128)(2,1)} async-done(((bf16[1024,1024]{1,0:T(8,128)(2,1)}), bf16[256,1024]{1,0:T(8,128)(2,1)}) %reduce-scatter.9.cloned.1.call-update) | async-done | bytes 524304 | tf_op jit(solution)/shard_map/reduce_scatter | solution.py:110
  251.2 2.0 fusion.26
  253.2 2.3 fusion.47
  255.8 5.0 convolution_convert_fusion.4
  260.8 2.8 convolution_convert_fusion.5
  263.6 2.8 convolution_convert_fusion.6
  266.4 34.6 %all-gather.8.cloned.1.call-done = bf16[1024,1024]{1,0:T(8,128)(2,1)} async-done(((bf16[256,1024]{1,0:T(8,128)(2,1)}), bf16[1024,1024]{1,0:T(8,128)(2,1)}) %all-gather.8.cloned.1.call-update) | async-done | bytes 2097168 | tf_op jit(solution)/shard_map/all_gather | solution.py:121
  301.0 3.8 fusion.48
  305.3 5.1 convolution_convert_fusion.7
  310.4 2.6 select_convert_fusion
  313.1 1.6 fusion.10
  314.7 2.9 fusion.9
  317.6 2.4 convolution_convert_fusion
  320.0 1.4 fusion.49
  321.4 1.1 copy-done.54
  322.6 1.5 convolution_convert_fusion.8
  324.1 1.0 copy-done.57
  325.1 5.3 convolution_convert_fusion.1
  330.5 1.3 copy-done.27
  331.8 4.6 convolution_convert_fusion.3
  336.4 99.4 %all-reduce.4.cloned.1.call-done = (bf16[1024,256]{1,0:T(8,128)(2,1)}, bf16[1024,256]{1,0:T(8,128)(2,1)}, bf16[1024,256]{1,0:T(8,128)(2,1)}, bf16[1024,256]{1,0:...) async-done(((bf16[1024,256]{1,0:T(8,128)(2,1)}, bf16[1024,256]{1,0:T(8,128)(2,1)}, ...) | async-done | bytes 6946832 | tf_op jit(solution)/shard_map/psum | solution.py:178
  435.8 2.2 convert_element_type.164
  438.0 2.1 convert_element_type.165
  440.1 1.0 convert_element_type.166
  441.2 1.0 convert_element_type.167
  442.2 1.1 convert_element_type.169
  443.3 1.9 convert_element_type.171
  445.3 1.9 convert_element_type.173
  447.3 1.9 convert_element_type.175
  449.3 32.9 %reduce-scatter.11.cloned.1.call-done = bf16[256,1024]{1,0:T(8,128)(2,1)} async-done(((bf16[1024,1024]{1,0:T(8,128)(2,1)}), bf16[256,1024]{1,0:T(8,128)(2,1)}) %reduce-scatter.11.cloned.1.call-update) | async-done | bytes 524304 | tf_op jit(solution)/shard_map/reduce_scatter | solution.py:164
  482.2 2.0 fusion.30
  484.2 42.2 %all-reduce = (f32[1024]{0:T(1024)}, f32[1024]{0:T(1024)}) all-reduce(f32[1024]{0:T(1024)S(1)} %get-tuple-element.14, f32[1024]{0:T(1024)S(1)} %copy-done.49), channel_id=1, replica_groups=mesh['dp'=8,'tensor'=4] {'dp','tensor'}, use_global_device_ids=true, to_apply=%region_19.20 | all-reduce | flops 2048 | bytes 16384 | tf_op jit(solution)/shard_map/psum | solution.py:197
  526.4 0.8 broadcast_multiply_fusion.2
  527.1 1.5 reduce-scatter.7.cloned.1.call-done
  528.7 3.1 fusion.21
  (146 shorter events, 6.4 us)
Async XLA Ops:
  7.2 192.7 %copy-start = (bf16[1024,704]{0,1:T(8,128)(2,1)S(1)}, bf16[1024,704]{0,1:T(8,128)(2,1)}, u32[]{:S(2)}) copy-start(bf16[1024,704]{0,1:T(8,128)(2,1)} %param.20) | copy-start | bytes 4325380
  7.2 4.2 copy-start.36
  7.2 4.2 copy-start.37
  7.2 4.3 copy-start.38
  7.2 52.9 %all-gather.4.cloned.1.call-start = ((), (), s32[]{:S(2)}) async-start(), calls=%async_computation.4 | async-start | bytes 2621440 | tf_op jit(solution)/shard_map/all_gather | solution.py:53
  11.3 1.0 copy-start.39
  11.3 2.4 copy-start.48
  11.3 107.5 %reduce-scatter.5.cloned.1.call-start = ((), (), s32[]{:S(2)}) async-start(), calls=%async_computation.5 | async-start | bytes 2621440 | tf_op jit(solution)/shard_map/reduce_scatter | solution.py:75
  12.4 1.3 copy-start.41
  14.3 51.7 %copy-start.31 = (pred[1024,1024]{1,0:T(8,128)(4,1)}, pred[1024,1024]{1,0:T(8,128)(4,1)S(1)}, u32[]{:S(2)}) copy-start(pred[1024,1024]{1,0:T(8,128)(4,1)S(1)} %fusion) | copy-start | bytes 3145732
  64.8 7.4 %copy-start.10 = (f32[1024,1024]{0,1:T(8,128)}, f32[1024,1024]{0,1:T(8,128)S(1)}, u32[]{:S(2)}) copy-start(f32[1024,1024]{0,1:T(8,128)S(1)} %fusion.50) | copy-start | bytes 12582916
  64.9 3.9 copy-start.11
  66.0 2.7 copy-start.15
  66.0 2.7 copy-start.17
  68.7 3.3 copy-start.2
  72.1 1.9 copy-start.40
  76.0 42.8 %copy-start.3 = (bf16[256,1024]{1,0:T(8,128)(2,1)S(1)}, bf16[256,1024]{1,0:T(8,128)(2,1)}, u32[]{:S(2)}) copy-start(bf16[256,1024]{1,0:T(8,128)(2,1)} %param.13) | copy-start | bytes 1572868
  76.1 106.2 %all-gather.6.cloned.1.call-start = ((), (), s32[]{:S(2)}) async-start(), calls=%async_computation.7 | async-start | bytes 2621440 | tf_op jit(solution)/shard_map/all_gather | solution.py:103
  76.8 174.4 %reduce-scatter.9.cloned.1.call-start = ((), (), s32[]{:S(2)}) async-start(), calls=%async_computation.8 | async-start | bytes 2621440 | tf_op jit(solution)/shard_map/reduce_scatter | solution.py:110
  120.1 49.8 %copy-start.45 = (f32[256]{0:T(256)}, f32[256]{0:T(256)S(1)}, u32[]{:S(2)}) copy-start(f32[256]{0:T(256)S(1)} %add_rsqrt_fusion.1) | copy-start | bytes 3076
  121.4 21.3 %collective-permute-start = (bf16[256,1024]{1,0:T(8,128)(2,1)S(1)}, bf16[256,1024]{1,0:T(8,128)(2,1)S(1)}, u32[]{:S(2)}, u32[]{:S(2)}) collective-permute-start(bf16[256,1024]{1,0:T(8,128)(2,1)S(1)} %multiply_convert_fusion.3), channel_id=1, source_target_pairs={{0,1},{1,2},{2,3},{3,0},{4,5},{5,6},{6,7},{7,4},{8,9},{9,10},{10,1... | collective-permute-start | bytes 1572872 | tf_op jit(solution)/shard_map/ppermute | solution.py:86
  143.5 26.4 %collective-permute-start.1 = (bf16[256,1024]{1,0:T(8,128)(2,1)S(1)}, bf16[256,1024]{1,0:T(8,128)(2,1)}, u32[]{:S(2)}, u32[]{:S(2)}) collective-permute-start(bf16[256,1024]{1,0:T(8,128)(2,1)S(1)} %collective-permute-done), channel_id=1, source_target_pairs={{0,1},{1,2},{2,3},{3,0},{4,5},{5,6},{6,7},{7,4},{8,9},{9,10},{10,1... | collective-permute-start | bytes 1572872 | tf_op jit(solution)/shard_map/ppermute | solution.py:86
  169.9 23.3 %collective-permute-start.2 = (bf16[256,1024]{1,0:T(8,128)(2,1)}, bf16[256,1024]{1,0:T(8,128)(2,1)}, u32[]{:S(2)}, u32[]{:S(2)}) collective-permute-start(bf16[256,1024]{1,0:T(8,128)(2,1)} %collective-permute-done.1), channel_id=1, source_target_pairs={{0,1},{1,2},{2,3},{3,0},{4,5},{5,6},{6,7},{7,4},{8,9},{9,10},{10,1... | collective-permute-start | bytes 1572872 | tf_op jit(solution)/shard_map/ppermute | solution.py:86
  185.9 9.5 %copy-start.20 = (bf16[256,1024]{1,0:T(8,128)(2,1)S(1)}, bf16[256,1024]{1,0:T(8,128)(2,1)}, u32[]{:S(2)}) copy-start(bf16[256,1024]{1,0:T(8,128)(2,1)} %copy-done.19) | copy-start | bytes 1572868
  195.5 2.4 copy-start.55
  197.9 1.9 copy-start.21
  202.9 1.9 copy-start.28
  202.9 1.9 copy-start.30
  208.1 43.1 %copy-start.4 = (bf16[256,1024]{1,0:T(8,128)(2,1)S(1)}, bf16[256,1024]{1,0:T(8,128)(2,1)}, u32[]{:S(2)}) copy-start(bf16[256,1024]{1,0:T(8,128)(2,1)} %reduce-scatter.5.cloned.1.call-done) | copy-start | bytes 1572868
  208.1 43.1 %copy-start.42 = (f32[1024]{0:T(1024)S(1)}, f32[1024]{0:T(1024)}, u32[]{:S(2)}) copy-start(f32[1024]{0:T(1024)} %param.24) | copy-start | bytes 12292
  208.1 43.1 %copy-start.46 = (f32[256]{0:T(256)S(1)}, f32[256]{0:T(256)}, u32[]{:S(2)}) copy-start(f32[256]{0:T(256)} %copy-done.45) | copy-start | bytes 3076
  208.1 45.1 %copy-start.5 = (bf16[256,1024]{1,0:T(8,128)(2,1)S(1)}, bf16[256,1024]{1,0:T(8,128)(2,1)}, u32[]{:S(2)}) copy-start(bf16[256,1024]{1,0:T(8,128)(2,1)} %param.25) | copy-start | bytes 1572868
  208.1 92.9 %all-gather.8.cloned.1.call-start = ((), (), s32[]{:S(2)}) async-start(), calls=%async_computation.9 | async-start | bytes 2621440 | tf_op jit(solution)/shard_map/all_gather | solution.py:121
  253.2 2.3 copy-start.51
  255.5 5.2 copy-start.29
  255.6 180.3 %all-reduce.4.cloned.1.call-start = ((), (), s32[]{:S(2)}) async-start(), calls=%async_computation.11 | async-start | bytes 13893632 | tf_op jit(solution)/shard_map/psum | solution.py:178
  255.8 5.0 copy-start.22
  260.8 2.8 copy-start.26
  260.8 2.8 copy-start.53
  263.6 37.4 %copy-start.9 = (f32[1,1024,4,64]{1,3,2,0:T(8,128)S(1)}, f32[1,1024,4,64]{1,3,2,0:T(8,128)}, u32[]{:S(2)}) copy-start(f32[1,1024,4,64]{1,3,2,0:T(8,128)} %copy-done.8) | copy-start | bytes 3145732
  304.7 12.9 %copy-start.56 = (bf16[1024,256]{0,1:T(8,128)(2,1)}, bf16[1024,256]{0,1:T(8,128)(2,1)S(1)}, u32[]{:S(2)}) copy-start(bf16[1024,256]{0,1:T(8,128)(2,1)S(1)} %get-tuple-element.27) | copy-start | bytes 1572868
  305.3 5.1 copy-start.12
  305.3 5.1 copy-start.32
  310.4 2.7 copy-start.18
  313.1 1.6 copy-start.16
  314.7 2.9 copy-start.52
  320.0 1.4 copy-start.14
  320.0 2.5 copy-start.54
  324.1 158.1 %reduce-scatter.11.cloned.1.call-start = ((), (), s32[]{:S(2)}) async-start(), calls=%async_computation.10 | async-start | bytes 2621440 | tf_op jit(solution)/shard_map/reduce_scatter | solution.py:164
  330.4 1.4 copy-start.27
  330.5 198.2 %reduce-scatter.7.cloned.1.call-start = ((), (), s32[]{:S(2)}) async-start(), calls=%async_computation.6 | async-start | bytes 2621440 | tf_op jit(solution)/shard_map/reduce_scatter | solution.py:95
  435.8 4.3 copy-start.35
  435.8 5.4 copy-start.34
  438.0 4.2 copy-start.33
  440.1 3.2 copy-start.25
  443.3 2.0 copy-start.24
  445.3 1.9 copy-start.23
  447.3 34.9 %copy-start.44 = (f32[1024]{0:T(1024)S(1)}, f32[1024]{0:T(1024)}, u32[]{:S(2)}) copy-start(f32[1024]{0:T(1024)} %param.23) | copy-start | bytes 12292
  447.3 36.9 %copy-start.49 = (f32[1024]{0:T(1024)S(1)}, f32[1024]{0:T(1024)}, u32[]{:S(2)}) copy-start(f32[1024]{0:T(1024)} %get-tuple-element.12) | copy-start | bytes 12292
  447.3 81.4 %copy-start.6 = (bf16[256,1024]{1,0:T(8,128)(2,1)S(1)}, bf16[256,1024]{1,0:T(8,128)(2,1)}, u32[]{:S(2)}) copy-start(bf16[256,1024]{1,0:T(8,128)(2,1)} %param.25) | copy-start | bytes 1572868
  447.3 81.4 %copy-start.7 = (bf16[256,1024]{1,0:T(8,128)(2,1)S(1)}, bf16[256,1024]{1,0:T(8,128)(2,1)}, u32[]{:S(2)}) copy-start(bf16[256,1024]{1,0:T(8,128)(2,1)} %reduce-scatter.9.cloned.1.call-done) | copy-start | bytes 1572868
  447.3 81.4 %copy-start.43 = (f32[1024]{0:T(1024)S(1)}, f32[1024]{0:T(1024)}, u32[]{:S(2)}) copy-start(f32[1024]{0:T(1024)} %param.24) | copy-start | bytes 12292
  447.3 81.4 %copy-start.47 = (f32[256]{0:T(256)S(1)}, f32[256]{0:T(256)}, u32[]{:S(2)}) copy-start(f32[256]{0:T(256)} %copy-done.45) | copy-start | bytes 3076
  526.3 5.5 %copy-start.1 = (bf16[1024,704]{0,1:T(8,128)(2,1)S(1)}, bf16[1024,704]{0,1:T(8,128)(2,1)}, u32[]{:S(2)}) copy-start(bf16[1024,704]{0,1:T(8,128)(2,1)} %param.20) | copy-start | bytes 4325380
  (5 other events, 4.2 us)
Sparse Core Ops, SparseCore 0:
  11.4 48.6 all-gather.3
  76.2 42.5 reduce-scatter.4
  120.5 61.7 all-gather.5
  208.2 42.9 reduce-scatter.8
  255.7 45.2 all-gather.7
  324.2 111.5 all-reduce.3
  438.2 43.9 reduce-scatter.10
  484.5 44.1 reduce-scatter.6
